TPU v7x, 32 devices: a whole 2x2x4 slice. The times are simulated.
32 devices in a mesh: layer: 8 (over z, x), land: 4 (over y, core).
Axes of the slice: x: 2, y: 2, z: 4, core: 2. Of those that a mesh axis runs over, the one named last changes fastest.
Arguments:
- gradients: bfloat16 [960, 65536], P(None, ('layer', 'land')), may hold values from -6 to 6
- queries: bfloat16 [32, 65536], P(None, ('layer', 'land')), may hold values from -6 to 6
- landmarks: bfloat16 [1024, 65536], P(None, ('layer', 'land')), may hold values from -0.0234375 to 0.0234375
- whitening: bfloat16 [1024, 1024], P(None, 'land'), may hold values from -2.5 to 2.5
Outputs:
- scores: float32 [32, 960], P('land', 'layer')
All inputs are finite; a program needn't handle non-finite values.
Results may differ from a plain program's by a relative error of at most 0.023.
Values may be sent and summed in bfloat16 or wider, within the bound.
A program may use at most 128 MiB of HBM per device.

v0:
```python
import jax
import jax.numpy as jnp
from jax import lax
from jax.sharding import PartitionSpec as P

LANDMARKS = 1024


def contract_rows(rows, piece):
    return lax.dot_general(
        rows, piece, (((1,), (1,)), ((), ())), preferred_element_type=jnp.float32
    )


def make_folder(example_rows, query_rows, piece):
    return (contract_rows(example_rows, piece), contract_rows(query_rows, piece))


def local(gradients, queries, landmarks, whitening):
    n_layer = lax.axis_size("layer")
    n_land = lax.axis_size("land")
    width = gradients.shape[1]
    rows_each = gradients.shape[0] // (n_layer * n_land)
    query_each = queries.shape[0] // (n_layer * n_land)
    split_ex = gradients.reshape(n_layer, n_land, rows_each, width)
    split_qr = queries.reshape(n_layer, n_land, query_each, width)
    moved_ex, moved_qr = (
        lax.all_to_all(split_ex, "land", split_axis=1, concat_axis=3, tiled=True),
        lax.all_to_all(split_qr, "land", split_axis=1, concat_axis=3, tiled=True),
    )
    layer_rows = moved_ex.reshape(n_layer * rows_each, n_land * width)
    layer_query = moved_qr.reshape(n_layer * query_each, n_land * width)
    partial_ex, partial_qr = make_folder(
        layer_rows, layer_query, lax.all_gather(landmarks, "land", axis=1, tiled=True)
    )
    share_ex, share_qr = (
        lax.psum_scatter(
            partial_ex.astype(jnp.bfloat16), "layer", scatter_dimension=0, tiled=True
        ).astype(jnp.float32),
        lax.psum_scatter(
            partial_qr.astype(jnp.bfloat16), "layer", scatter_dimension=0, tiled=True
        ).astype(jnp.float32),
    )
    projected, query_proj = (
        lax.all_gather(share_ex.astype(jnp.bfloat16), "land", axis=0, tiled=True),
        lax.all_gather(share_qr.astype(jnp.bfloat16), "land", axis=0, tiled=True),
    )
    whitened = jnp.dot(projected, whitening, preferred_element_type=jnp.float32).astype(
        jnp.bfloat16
    )
    query_white = jnp.dot(query_proj, whitening, preferred_element_type=jnp.float32).astype(
        jnp.bfloat16
    )
    all_queries = lax.all_gather(query_white, "layer", axis=0, tiled=True)
    factor = LANDMARKS ** (-0.5)
    return lax.psum_scatter(
        (contract_rows(all_queries, whitened) * factor).astype(jnp.bfloat16),
        "land",
        scatter_dimension=0,
        tiled=True,
    ).astype(jnp.float32)


def solution(mesh):
    return jax.shard_map(
        local,
        mesh=mesh,
        in_specs=(
            P(None, ("layer", "land")),
            P(None, ("layer", "land")),
            P(None, ("layer", "land")),
            P(None, "land"),
        ),
        out_specs=P("land", "layer"),
        check_vma=False,
    )
```

profile of v0, /device:TPU:0, one launch (start us, length us, event | category | flops | bytes accessed | tf_op | source)
XLA Modules:
  0.0 296.0 jit_solution(8832669708729953579)
XLA Ops:
  6.5 0.0 copy-start
  6.5 0.0 all-gather.5.cloned.1.call-start
  6.5 0.7 all-gather.5.cloned.1.call-update
  7.3 5.0 %reshape.19 = bf16[8,4,30,2048]{3,2,1,0:T(8,128)(2,1)} reshape(bf16[960,2048]{1,0:T(8,128)(2,1)} %param.4) | data formatting | bytes 7864320 | tf_op jit(solution)/shard_map/reshape | solution.py:25
  12.3 6.4 %copy.9 = bf16[8,4,30,2048]{3,0,2,1:T(8,128)(2,1)} copy(bf16[8,4,30,2048]{3,2,1,0:T(8,128)(2,1)} %reshape.19) | data formatting | bytes 7864320 | tf_op jit(solution)/shard_map/reshape | solution.py:25
  18.7 0.0 copy-start.1
  18.7 0.0 copy-start.3
  18.7 0.0 copy-start.2
  18.7 5.1 %all-to-all-start.1 = ((bf16[8,4,30,2048]{3,0,2,1:T(8,128)(2,1)}), bf16[8,4,30,2048]{3,0,2,1:T(8,128)(2,1)}, u32[]{:S(2)}, u32[]{:S(2)}) async-start(bf16[8,4,30,2048]{3,0,2,1:T(8,128)(2,1)} %copy.9), calls=%async_computation.1 | async-start | bytes 7864320 | tf_op jit(solution)/shard_map/all_to_all | solution.py:28
  23.8 0.0 copy-done.1
  23.8 0.1 reshape.17
  23.9 0.7 copy.8
  24.6 0.0 copy-done.3
  24.6 0.6 dynamic-slice.4
  25.2 0.0 copy-done.2
  25.2 0.7 fusion.7
  27.1 85.5 %all-to-all-done.1 = bf16[8,4,30,2048]{3,0,2,1:T(8,128)(2,1)} async-done(((bf16[8,4,30,2048]{3,0,2,1:T(8,128)(2,1)}), bf16[8,4,30,2048]{3,0,2,1:T(8,128)(2,1)}, u32[]{:S(2)}, u32[]{:S(2)}) %all-to-all-start.1) | async-done | bytes 3932192 | tf_op jit(solution)/shard_map/all_to_all | solution.py:28
  112.6 3.5 %all-to-all-start = ((bf16[8,4,1,2048]{3,0,2,1:T(8,128)(2,1)}), bf16[8,4,1,2048]{3,0,2,1:T(8,128)(2,1)S(1)}, u32[]{:S(2)}, u32[]{:S(2)}) async-start(bf16[8,4,1,2048]{3,0,2,1:T(8,128)(2,1)} %copy.8), calls=%async_computation | async-start | bytes 262144 | tf_op jit(solution)/shard_map/all_to_all | solution.py:29
  116.1 5.1 %copy.10 = bf16[8,1,30,4,2048]{4,3,2,0,1:T(4,128)(2,1)S(1)} copy(bf16[8,1,30,4,2048]{4,0,2,3,1:T(8,128)(2,1)} %bitcast.4) | data formatting | bytes 7864320 | tf_op jit(solution)/shard_map/all_to_all | solution.py:28
  121.2 6.0 %copy.12 = bf16[30,8,4,2048]{3,1,2,0:T(8,128)(2,1)} copy(bf16[30,8,4,2048]{3,2,1,0:T(4,128)(2,1)S(1)} %bitcast.29) | data formatting | bytes 7864320
  127.2 33.9 %all-gather.5.cloned.1.call-done = bf16[1024,8192]{1,0:T(8,128)(2,1)} async-done(((bf16[1024,2048]{1,0:T(8,128)(2,1)}), bf16[1024,8192]{1,0:T(8,128)(2,1)}) %all-gather.5.cloned.1.call-update) | async-done | bytes 16777232 | tf_op jit(solution)/shard_map/all_gather | solution.py:34
  161.1 11.5 %convolution_convert_fusion = bf16[240,1024]{1,0:T(8,128)(2,1)S(1)} fusion(bf16[240,8192]{1,0:T(8,128)(2,1)} %bitcast.30, bf16[1024,8192]{1,0:T(8,128)(2,1)} %all-gather.5.cloned.1.call-done), kind=kOutput, calls=%fused_computation | convolution fusion | flops 4026777600 | bytes 21200896 | tf_op jit(solution)/shard_map/dot_general | solution.py:10
  172.6 25.3 %fusion = bf16[32,1024]{1,0:T(8,128)(2,1)S(1)} fusion(bf16[240,1024]{1,0:T(8,128)(2,1)S(1)} %convolution_convert_fusion), kind=kCustom, calls=%all-reduce-scatter | all-reduce-scatter fusion | flops 262145 | bytes 557568
  197.9 2.1 collective-permute-start
  200.0 0.0 all-to-all-done
  200.0 10.2 %convolution_convert_fusion.2 = bf16[8,1024]{1,0:T(8,128)(2,1)S(1)} fusion(bf16[8,8192]{1,0:T(8,128)(2,1)S(1)} %bitcast.31, bf16[1024,8192]{1,0:T(8,128)(2,1)} %all-gather.5.cloned.1.call-done), kind=kOutput, calls=%fused_computation.3 | convolution fusion | flops 134225920 | bytes 16924672 | tf_op jit(solution)/shard_map/dot_general | solution.py:10
  210.2 33.6 %all-reduce = bf16[8,1024]{1,0:T(8,128)(2,1)S(1)} all-reduce(bf16[8,1024]{1,0:T(8,128)(2,1)S(1)} %convolution_convert_fusion.2), channel_id=2, replica_groups=mesh['layer'=8,'land'=4] {'layer'}, use_global_device_ids=true, to_apply=%region_0.0.clone | all-reduce | flops 8192 | bytes 32768
  243.8 0.6 dynamic-slice_bitcast_fusion.1
  244.4 5.2 %all-gather = bf16[4,1,1024]{2,1,0:T(2,128)(2,1)S(1)} all-gather(bf16[1,1,1024]{2,1,0:T(2,128)(2,1)S(1)} %dynamic-slice_bitcast_fusion.1), channel_id=1, replica_groups=mesh['layer'=8,'land'=4] {'land'}, dimensions={0}, use_global_device_ids=true | all-gather | bytes 10240 | tf_op jit(solution)/shard_map/all_gather | solution.py:46
  249.6 0.0 copy-done
  249.6 0.2 fusion.4
  249.8 26.0 %all-gather.1 = bf16[8,4,256]{2,1,0:T(4,128)(2,1)S(1)} all-gather(bf16[1,4,256]{2,1,0:T(4,128)(2,1)S(1)} %fusion.4), channel_id=1, replica_groups=mesh['layer'=8,'land'=4] {'layer'}, dimensions={0}, use_global_device_ids=true | all-gather | bytes 18432 | tf_op jit(solution)/shard_map/all_gather | solution.py:54
  275.8 0.0 collective-permute-done
  275.8 0.2 concatenate
  276.1 5.8 %all-gather.2 = bf16[4,30,1024]{2,1,0:T(8,128)(2,1)S(1)} all-gather(bf16[1,30,1024]{2,1,0:T(8,128)(2,1)S(1)} %dynamic-slice_bitcast_fusion), channel_id=1, replica_groups=mesh['layer'=8,'land'=4] {'land'}, dimensions={0}, use_global_device_ids=true | all-gather | bytes 307200 | tf_op jit(solution)/shard_map/all_gather | solution.py:45
  281.9 0.1 reshape.26
  281.9 0.3 fusion.3
  282.3 6.2 %all-reduce.2 = bf16[32,120]{1,0:T(8,128)(2,1)S(1)} all-reduce(bf16[32,120]{1,0:T(8,128)(2,1)S(1)} %fusion.3), channel_id=4, replica_groups=mesh['layer'=8,'land'=4] {'land'}, use_global_device_ids=true, to_apply=%region_2.0.clone | all-reduce | flops 3840 | bytes 15360
  288.5 0.6 dynamic-slice_convert_fusion
  (3 shorter events, 0.1 us)
Async XLA Ops:
  6.5 243.1 %copy-start = (bf16[1024,256]{1,0:T(8,128)(2,1)S(1)}, bf16[1024,256]{1,0:T(8,128)(2,1)}, u32[]{:S(2)}) copy-start(bf16[1024,256]{1,0:T(8,128)(2,1)} %param.7) | copy-start | bytes 1572868
  6.5 154.6 %all-gather.5.cloned.1.call-start = ((), (), s32[]{:S(2)}) async-start(), calls=%async_computation.2 | async-start | bytes 20971520 | tf_op jit(solution)/shard_map/all_gather | solution.py:34
  18.7 5.1 %copy-start.1 = (bf16[32,2048]{1,0:T(8,128)(2,1)S(1)}, bf16[32,2048]{1,0:T(8,128)(2,1)}, u32[]{:S(2)}) copy-start(bf16[32,2048]{1,0:T(8,128)(2,1)} %param.5) | copy-start | bytes 393220
  18.7 6.0 %copy-start.3 = (u32[32]{0:T(128)S(1)}, u32[32]{0:T(128)}, u32[]{:S(2)}) copy-start(u32[32]{0:T(128)} %constant.12) | copy-start | bytes 388
  18.7 6.5 %copy-start.2 = (u32[32]{0:T(128)S(1)}, u32[32]{0:T(128)}, u32[]{:S(2)}) copy-start(u32[32]{0:T(128)} %constant.4) | copy-start | bytes 388
  18.7 93.9 %all-to-all-start.1 = ((bf16[8,4,30,2048]{3,0,2,1:T(8,128)(2,1)}), bf16[8,4,30,2048]{3,0,2,1:T(8,128)(2,1)}, u32[]{:S(2)}, u32[]{:S(2)}) async-start(bf16[8,4,30,2048]{3,0,2,1:T(8,128)(2,1)} %copy.9), calls=%async_computation.1 | async-start | bytes 7864320 | tf_op jit(solution)/shard_map/all_to_all | solution.py:28
  112.6 87.4 %all-to-all-start = ((bf16[8,4,1,2048]{3,0,2,1:T(8,128)(2,1)}), bf16[8,4,1,2048]{3,0,2,1:T(8,128)(2,1)S(1)}, u32[]{:S(2)}, u32[]{:S(2)}) async-start(bf16[8,4,1,2048]{3,0,2,1:T(8,128)(2,1)} %copy.8), calls=%async_computation | async-start | bytes 262144 | tf_op jit(solution)/shard_map/all_to_all | solution.py:29
  197.9 77.9 %collective-permute-start = (bf16[14,1024]{1,0:T(8,128)(2,1)S(1)}, bf16[14,1024]{1,0:T(8,128)(2,1)S(1)}, u32[]{:S(2)}, u32[]{:S(2)}) collective-permute-start(bf16[14,1024]{1,0:T(8,128)(2,1)S(1)} %slice), channel_id=1, source_target_pairs={{0,4},{4,8},{8,12},{12,16},{16,20},{20,24},{24,28},{1,5},{5,9},{9,... | collective-permute-start | bytes 86024
Sparse Core Ops, SparseCore 0:
  8.9 152.1 all-gather.4
where the time goes:
time: 297 us; the launch traced here: 296 us
  waiting for transfers between devices  120 us (40%)
  blocking collectives  102 us (34%)
  local copies, waits for them, and re-layouts  25.6 us (9%)
  matrix products  22.2 us (7%)
  between operations  14.8 us (5%)
  starting transfers between devices  10.7 us (4%)
    all_to_all x1, waiting for transfers between devices, local(): lax.all_to_all(split_ex, 'land', split_axis=1, concat_axis=3, tiled=True)  85.5 us
    unnamed x3, blocking collectives  65.1 us
    all_gather x1, waiting for transfers between devices, local(): lax.all_gather(landmarks, 'land', axis=1, tiled=True)  33.9 us
    all_gather x1, blocking collectives, local(): all_queries = lax.all_gather(query_white, 'layer', axis=0, tiled=True)  26 us
    dot_general x3, matrix products, contract_rows(): lax.dot_general(rows, piece, (((1,), (1,)), ((), ())), preferred_element_...  22 us
    reshape x2, local copies, waits for them, and re-layouts, local(): split_ex = gradients.reshape(n_layer, n_land, rows_each, width)  11.4 us
    unnamed x17, local copies, waits for them, and re-layouts  8.18 us
  transfers between devices with their start and end apart: 4, of which 2 were waited for; matrix products, arithmetic and copies ran while one was open for 24% of the time, Pallas kernels for 0%

commit v1 on v0

v1 whole, which is shorter than its diff:
```python
import jax
import jax.numpy as jnp
from jax import lax
from jax.sharding import PartitionSpec as P

NN = (((1,), (0,)), ((), ()))
NT = (((1,), (1,)), ((), ()))


def dot(a, b, dims):
    return lax.dot_general(a, b, dims, preferred_element_type=jnp.float32)


def local(gradients, queries, landmarks, whitening):
    half = jnp.bfloat16
    factor = landmarks.shape[0] ** (-0.5)
    partial = dot(queries, landmarks, NT).astype(half)
    query_proj = lax.psum(partial, ("layer", "land"))
    query_white = dot(query_proj, whitening, NN).astype(half)
    back = lax.psum(dot(query_white, whitening, NT).astype(half), "land")
    spread = dot(back, landmarks, NN).astype(half)
    scores = dot(spread, gradients, NT) * factor
    share = lax.psum_scatter(
        scores.astype(half), "layer", scatter_dimension=1, tiled=True
    )
    return lax.psum_scatter(share, "land", scatter_dimension=0, tiled=True).astype(
        jnp.float32
    )


def solution(mesh):
    return jax.shard_map(
        local,
        mesh=mesh,
        in_specs=(
            P(None, ("layer", "land")),
            P(None, ("layer", "land")),
            P(None, ("layer", "land")),
            P(None, "land"),
        ),
        out_specs=P("land", "layer"),
        check_vma=False,
    )
```

time: 297 us -> 224 us (0.75)
  blocking collectives: 102 us -> 43.6 us
  waiting for transfers between devices: 120 us -> 152 us
  local copies, waits for them, and re-layouts: 25.6 us -> 1.26 us
  starting transfers between devices: 10.7 us -> 0.04 us
  matrix products: 22.2 us -> 11.6 us
    psum x0 -> x2, waiting for transfers between devices: none -> 152 us  [the longest x1 122 us: local(): query_proj = lax.psum(partial, ('layer', 'land'))]
    all_to_all x2 -> x0, waiting for transfers between devices: 85.5 us -> none  [the longest x1 85.5 us: local(): lax.all_to_all(split_ex, 'land', split_axis=1, concat_axis=3, tiled=True)]
    all_gather x3 -> x0, blocking collectives: 37 us -> none  [the longest x1 26 us: local(): all_queries = lax.all_gather(query_white, 'layer', axis=0, tiled=True)]
    all_gather x1 -> x0, waiting for transfers between devices: 33.9 us -> none  [local(): lax.all_gather(landmarks, 'land', axis=1, tiled=True)]
    unnamed x3 -> x2, blocking collectives: 65.1 us -> 43.6 us
    reshape x4 -> x0, local copies, waits for them, and re-layouts: 12.2 us -> none  [the longest x2 11.4 us: local(): split_ex = gradients.reshape(n_layer, n_land, rows_each, width)]
    dot_general x4 -> x3, matrix products: 22.2 us -> 11.6 us  [dot(): return lax.dot_general(a, b, dims, preferred_element_type=jnp.float32)]
    all_to_all x2 -> x0, starting transfers between devices: 8.62 us -> none  [the longest x1 5.12 us: local(): lax.all_to_all(split_ex, 'land', split_axis=1, concat_axis=3, tiled=True)]
  transfers between devices with their start and end apart: 4 -> 2, of which waited for: 2 -> 2; matrix products, arithmetic and copies ran while one was open for 24% -> 1% of each run, Pallas kernels for 0% -> 0%
where the time goes in v1:
time: 224 us
  waiting for transfers between devices  152 us (68%)
  blocking collectives  43.6 us (19%)
  between operations  14.7 us (7%)
  matrix products  11.6 us (5%)
    psum x1, waiting for transfers between devices, local(): query_proj = lax.psum(partial, ('layer', 'land'))  122 us
    unnamed x2, blocking collectives  43.6 us
    psum x1, waiting for transfers between devices, local(): back = lax.psum(dot(query_white, whitening, NT).astype(half), 'land')  29.8 us
    dot_general x3, matrix products, dot(): return lax.dot_general(a, b, dims, preferred_element_type=jnp.float32)  11.6 us
  transfers between devices with their start and end apart: 2, of which 2 were waited for; matrix products, arithmetic and copies ran while one was open for 1% of the time, Pallas kernels for 0%

profile of v1, /device:TPU:0, one launch (start us, length us, event | category | flops | bytes accessed | tf_op | source)
XLA Modules:
  0.0 224.0 jit_solution(2773502246041843266)
XLA Ops:
  6.5 0.0 copy-start
  6.5 0.0 copy-start.2
  6.5 0.0 copy-start.1
  6.5 0.0 all-reduce.5.cloned.1.call-start
  6.5 4.3 %convolution_convert_fusion.2 = bf16[32,1024]{1,0:T(8,128)(2,1)} fusion(bf16[32,2048]{1,0:T(8,128)(2,1)} %param.5, bf16[1024,2048]{1,0:T(8,128)(2,1)} %param.6), kind=kOutput, calls=%fused_computation.5 | convolution fusion | flops 134250496 | bytes 4390912 | tf_op jit(solution)/shard_map/dot_general | solution.py:11
  10.8 0.0 all-reduce.5.cloned.1.call-update
  10.9 0.0 all-reduce.7.cloned.1.call-start
  10.9 122.3 %all-reduce.5.cloned.1.call-done = bf16[32,1024]{1,0:T(8,128)(2,1)} async-done(((bf16[32,1024]{1,0:T(8,128)(2,1)}), bf16[32,1024]{1,0:T(8,128)(2,1)}) %all-reduce.5.cloned.1.call-update) | async-done | bytes 65552 | tf_op jit(solution)/shard_map/psum | solution.py:18
  133.2 0.0 copy-done
  133.2 2.0 convolution_convert_fusion.1
  135.2 0.0 all-reduce.7.cloned.1.call-update
  135.2 0.0 copy-done.2
  135.2 0.6 dynamic-slice
  135.8 0.0 copy-done.1
  135.8 0.6 dynamic-slice.2
  137.6 29.8 %all-reduce.7.cloned.1.call-done = bf16[32,1024]{1,0:T(8,128)(2,1)} async-done(((bf16[32,1024]{1,0:T(8,128)(2,1)}), bf16[32,1024]{1,0:T(8,128)(2,1)}) %all-reduce.7.cloned.1.call-update) | async-done | bytes 65552 | tf_op jit(solution)/shard_map/psum | solution.py:20
  167.4 5.4 %fusion.2 = bf16[32,960]{1,0:T(8,128)(2,1)S(1)} fusion(bf16[960,2048]{1,0:T(8,128)(2,1)} %param.4, bf16[32,1024]{1,0:T(8,128)(2,1)} %all-reduce.7.cloned.1.call-done, bf16[1024,2048]{1,0:T(8,128)(2,1)} %param.6), kind=kOutput, calls=%fused_computation.3 | convolution fusion | flops 260173824 | bytes 8253440 | tf_op jit(solution)/shard_map/dot_general | solution.py:11
  172.8 37.5 %all-reduce = bf16[32,960]{1,0:T(8,128)(2,1)S(1)} all-reduce(bf16[32,960]{1,0:T(8,128)(2,1)S(1)} %fusion.2), channel_id=2, replica_groups=mesh['layer'=8,'land'=4] {'layer'}, use_global_device_ids=true, to_apply=%region_2.0.clone | all-reduce | flops 30720 | bytes 122880
  210.3 0.1 constant_dynamic-slice_fusion
  210.4 6.1 %all-reduce.1 = bf16[32,120]{1,0:T(8,128)(2,1)S(1)} all-reduce(bf16[32,120]{1,0:T(8,128)(2,1)S(1)} %constant_dynamic-slice_fusion), channel_id=3, replica_groups=mesh['layer'=8,'land'=4] {'land'}, use_global_device_ids=true, to_apply=%region_3.0.clone | all-reduce | flops 3840 | bytes 15360
  216.5 0.6 dynamic-slice_convert_fusion
Async XLA Ops:
  6.5 126.7 %copy-start = (bf16[1024,256]{1,0:T(8,128)(2,1)S(1)}, bf16[1024,256]{1,0:T(8,128)(2,1)}, u32[]{:S(2)}) copy-start(bf16[1024,256]{1,0:T(8,128)(2,1)} %param.7) | copy-start | bytes 1572868
  6.5 128.7 %copy-start.2 = (u32[32]{0:T(128)S(1)}, u32[32]{0:T(128)}, u32[]{:S(2)}) copy-start(u32[32]{0:T(128)} %constant.4) | copy-start | bytes 388
  6.5 129.3 %copy-start.1 = (u32[32]{0:T(128)S(1)}, u32[32]{0:T(128)}, u32[]{:S(2)}) copy-start(u32[32]{0:T(128)} %constant.8) | copy-start | bytes 388
  6.5 126.7 %all-reduce.5.cloned.1.call-start = ((), (), s32[]{:S(2)}) async-start(), calls=%async_computation | async-start | bytes 131072 | tf_op jit(solution)/shard_map/psum | solution.py:18
  10.9 156.6 %all-reduce.7.cloned.1.call-start = ((), (), s32[]{:S(2)}) async-start(), calls=%async_computation.1 | async-start | bytes 131072 | tf_op jit(solution)/shard_map/psum | solution.py:20
Sparse Core Ops, SparseCore 0:
  12.9 120.2 all-reduce.4
  135.5 31.8 all-reduce.6

commit v2 on v1

v2 whole, which is shorter than its diff:
```python
import functools
import jax
import jax.numpy as jnp
from jax import lax
from jax.experimental import pallas as pl
from jax.experimental.pallas import tpu as pltpu
from jax.sharding import PartitionSpec as P

NN = (((1,), (0,)), ((), ()))
NT = (((1,), (1,)), ((), ()))
HALF = jnp.bfloat16
FULL = jnp.float32


def dot(a, b, dims):
    return lax.dot_general(a, b, dims, preferred_element_type=FULL)


def kernel(
    n_layer, n_land, factor,
    g_hbm, q_hbm, l_hbm, w_hbm, out_ref,
    g_buf, q_buf, l_buf, w_buf, load_sem,
    qs, qr, hs, hr, us, ur, bs, br, ss, sr, fs, fr,
    layer_send, layer_recv, land_send, land_recv,
):
    layer = lax.axis_index("layer")
    land = lax.axis_index("land")
    n_blocks = l_buf.shape[0]

    loads = [pltpu.make_async_copy(q_hbm, q_buf, load_sem.at[0])]
    for b in range(n_blocks):
        loads.append(pltpu.make_async_copy(l_hbm.at[b], l_buf.at[b], load_sem.at[1 + b]))
    loads.append(pltpu.make_async_copy(w_hbm, w_buf, load_sem.at[1 + n_blocks]))
    loads.append(pltpu.make_async_copy(g_hbm, g_buf, load_sem.at[2 + n_blocks]))
    for load in loads:
        load.start()

    def layer_peer(k):
        return lax.rem(layer + k, n_layer)

    def land_peer(k):
        return lax.rem(land + k, n_land)

    barrier = pltpu.get_barrier_semaphore()
    for k in range(1, n_layer):
        pl.semaphore_signal(barrier, inc=1, device_id=(layer_peer(k), land),
                            device_id_type=pl.DeviceIdType.MESH)
    for k in range(1, n_land):
        pl.semaphore_signal(barrier, inc=1, device_id=(layer, land_peer(k)),
                            device_id_type=pl.DeviceIdType.MESH)

    def over_layer(phase, source, target):
        copies = []
        for k in range(1, n_layer):
            peer = layer_peer(k)
            copy = pltpu.make_async_remote_copy(
                src_ref=source(peer), dst_ref=target(k),
                send_sem=layer_send.at[phase, k - 1],
                recv_sem=layer_recv.at[phase, k - 1],
                device_id=(peer, land), device_id_type=pl.DeviceIdType.MESH)
            copy.start()
            copies.append(copy)
        return copies

    def over_land(phase, source, target):
        copies = []
        for k in range(1, n_land):
            peer = land_peer(k)
            copy = pltpu.make_async_remote_copy(
                src_ref=source(peer), dst_ref=target(k),
                send_sem=land_send.at[phase, k - 1],
                recv_sem=land_recv.at[phase, k - 1],
                device_id=(layer, peer), device_id_type=pl.DeviceIdType.MESH)
            copy.start()
            copies.append(copy)
        return copies

    sent = []

    loads[0].wait()
    rows = qs.shape[1]
    width = l_buf.shape[1]
    for b in range(n_blocks):
        loads[1 + b].wait()
        part = dot(q_buf[...], l_buf[b], NT)
        for i in range(n_layer):
            qs[i, :, b * width:(b + 1) * width] = part[i * rows:(i + 1) * rows].astype(HALF)

    pl.semaphore_wait(barrier, n_layer + n_land - 2)

    copies = over_layer(0, lambda p: qs.at[p], lambda k: qr.at[k - 1])
    total = qs[layer].astype(FULL)
    for k, copy in enumerate(copies):
        copy.wait_recv()
        total += qr[k].astype(FULL)
    sent += copies

    hs[...] = total
    copies = over_land(0, lambda p: hs, lambda k: hr.at[k - 1])
    for k, copy in enumerate(copies):
        copy.wait_recv()
        total += hr[k]
    sent += copies

    loads[1 + n_blocks].wait()
    white = dot(total.astype(HALF), w_buf[...], NN).astype(HALF)
    back = dot(white, w_buf[...], NT)
    us[...] = back
    copies = over_land(1, lambda p: us, lambda k: ur.at[k - 1])
    for k, copy in enumerate(copies):
        copy.wait_recv()
        back += ur[k]
    sent += copies

    bs[...] = back.astype(HALF)
    copies = over_layer(1, lambda p: bs, lambda k: br.at[layer])
    br[layer] = bs[...]
    loads[2 + n_blocks].wait()
    for copy in copies:
        copy.wait_recv()
    sent += copies

    folded = jnp.concatenate([br[i].astype(FULL) for i in range(n_layer)], axis=0).astype(HALF)
    spread = jnp.zeros((folded.shape[0], l_buf.shape[2]), FULL)
    for b in range(n_blocks):
        spread += dot(folded[:, b * width:(b + 1) * width], l_buf[b], NN)
    spread = spread.astype(HALF)

    for i in range(n_layer):
        ss[i] = (dot(spread, g_buf[i], NT) * factor).astype(HALF)
    copies = over_layer(2, lambda p: ss.at[p], lambda k: sr.at[k - 1])
    score = ss[layer].astype(FULL)
    for k, copy in enumerate(copies):
        copy.wait_recv()
        score += sr[k].astype(FULL)
    sent += copies

    share = fs.shape[1]
    for j in range(n_land):
        fs[j] = score[j * share:(j + 1) * share]
    copies = over_land(2, lambda p: fs.at[p], lambda k: fr.at[k - 1])
    result = fs[land]
    for k, copy in enumerate(copies):
        copy.wait_recv()
        result += fr[k]
    sent += copies
    out_ref[...] = result

    for copy in sent:
        copy.wait_send()


def fused(gradients, queries, landmarks, whitening):
    n_layer = lax.axis_size("layer")
    n_land = lax.axis_size("land")
    n_rows, width = gradients.shape
    n_query = queries.shape[0]
    n_mark = landmarks.shape[0]
    n_blocks = 4
    each, rows, share = n_rows // n_layer, n_query // n_layer, n_query // n_land
    any_space = pl.BlockSpec(memory_space=pl.ANY)
    return pl.pallas_call(
        functools.partial(kernel, n_layer, n_land, n_mark ** (-0.5)),
        out_shape=jax.ShapeDtypeStruct((share, each), FULL),
        in_specs=[any_space] * 4,
        out_specs=pl.BlockSpec(memory_space=pltpu.VMEM),
        scratch_shapes=[
            pltpu.VMEM((n_layer, each, width), HALF),
            pltpu.VMEM((n_query, width), HALF),
            pltpu.VMEM((n_blocks, n_mark // n_blocks, width), HALF),
            pltpu.VMEM(whitening.shape, HALF),
            pltpu.SemaphoreType.DMA((n_blocks + 3,)),
            pltpu.VMEM((n_layer, rows, n_mark), HALF),
            pltpu.VMEM((n_layer - 1, rows, n_mark), HALF),
            pltpu.VMEM((rows, n_mark), FULL),
            pltpu.VMEM((n_land - 1, rows, n_mark), FULL),
            pltpu.VMEM((rows, n_mark), FULL),
            pltpu.VMEM((n_land - 1, rows, n_mark), FULL),
            pltpu.VMEM((rows, n_mark), HALF),
            pltpu.VMEM((n_layer, rows, n_mark), HALF),
            pltpu.VMEM((n_layer, n_query, each), HALF),
            pltpu.VMEM((n_layer - 1, n_query, each), HALF),
            pltpu.VMEM((n_land, share, each), FULL),
            pltpu.VMEM((n_land - 1, share, each), FULL),
            pltpu.SemaphoreType.DMA((3, n_layer - 1)),
            pltpu.SemaphoreType.DMA((3, n_layer - 1)),
            pltpu.SemaphoreType.DMA((3, n_land - 1)),
            pltpu.SemaphoreType.DMA((3, n_land - 1)),
        ],
        compiler_params=pltpu.CompilerParams(
            collective_id=0, has_side_effects=True, vmem_limit_bytes=48 << 20
        ),
    )(
        gradients.reshape(n_layer, each, width),
        queries,
        landmarks.reshape(n_blocks, n_mark // n_blocks, width),
        whitening,
    )


def staged(gradients, queries, landmarks, whitening):
    factor = landmarks.shape[0] ** (-0.5)
    partial = dot(queries, landmarks, NT).astype(HALF)
    query_proj = lax.psum(partial, ("layer", "land"))
    query_white = dot(query_proj, whitening, NN).astype(HALF)
    back = lax.psum(dot(query_white, whitening, NT).astype(HALF), "land")
    spread = dot(back, landmarks, NN).astype(HALF)
    scores = dot(spread, gradients, NT) * factor
    share = lax.psum_scatter(
        scores.astype(HALF), "layer", scatter_dimension=1, tiled=True
    )
    return lax.psum_scatter(share, "land", scatter_dimension=0, tiled=True).astype(FULL)


def local(gradients, queries, landmarks, whitening):
    held = 2 * (gradients.size + queries.size + landmarks.size + whitening.size)
    few = lax.axis_size("layer") * lax.axis_size("land") <= 64
    if few and held <= (24 << 20) and gradients.shape[1] % 128 == 0:
        return fused(gradients, queries, landmarks, whitening)
    return staged(gradients, queries, landmarks, whitening)


def solution(mesh):
    return jax.shard_map(
        local,
        mesh=mesh,
        in_specs=(
            P(None, ("layer", "land")),
            P(None, ("layer", "land")),
            P(None, ("layer", "land")),
            P(None, "land"),
        ),
        out_specs=P("land", "layer"),
        check_vma=False,
    )
```

time: 224 us -> 36.9 us (0.16)
  waiting for transfers between devices: 152 us -> 0 us
  blocking collectives: 43.6 us -> 0 us
  Pallas kernels: 0 us -> 32 us
  between operations: 14.7 us -> 0.01 us
  matrix products: 11.6 us -> 0 us
  local copies, waits for them, and re-layouts: 1.26 us -> 4.65 us
    psum x2 -> x0, waiting for transfers between devices: 152 us -> none  [the longest x1 122 us: local(): query_proj = lax.psum(partial, ('layer', 'land'))]
    unnamed x2 -> x0, blocking collectives: 43.6 us -> none
    pallas_call x0 -> x1, Pallas kernels: none -> 32 us  [fused(): pl.pallas_call(functools.partial(kernel, n_layer, n_land, n_mark ** (-0.5...]
    dot_general x3 -> x0, matrix products: 11.6 us -> none  [dot(): return lax.dot_general(a, b, dims, preferred_element_type=jnp.float32)]
    unnamed x9 -> x7, local copies, waits for them, and re-layouts: 1.26 us -> 4.65 us
  transfers between devices with their start and end apart: 2 -> 0, of which waited for: 2 -> 0; matrix products, arithmetic and copies ran while one was open for 1% -> 0% of each run, Pallas kernels for 0% -> 0%
where the time goes in v2:
time: 36.9 us; the launch traced here: 36.7 us
  Pallas kernels  32 us (87%)
  local copies, waits for them, and re-layouts  4.65 us (13%)
    pallas_call x1, Pallas kernels, fused(): pl.pallas_call(functools.partial(kernel, n_layer, n_land, n_mark ** (-0.5...  32 us
    unnamed x7, local copies, waits for them, and re-layouts  4.65 us

profile of v2, /device:TPU:0, one launch (start us, length us, event | category | flops | bytes accessed | tf_op | source)
XLA Modules:
  0.0 36.7 jit_solution(10637138097328538199)
XLA Ops:
  0.0 0.0 copy-start
  0.0 2.1 %copy-done = bf16[960,2048]{1,0:T(8,128)(2,1)S(1)} copy-done((bf16[960,2048]{1,0:T(8,128)(2,1)S(1)}, bf16[960,2048]{1,0:T(8,128)(2,1)}, u32[]{:S(2)}) %copy-start) | copy-done | bytes 3932184
  2.1 0.0 copy-start.1
  2.1 1.0 %copy-done.1 = bf16[1024,256]{1,0:T(8,128)(2,1)S(1)} copy-done((bf16[1024,256]{1,0:T(8,128)(2,1)S(1)}, bf16[1024,256]{1,0:T(8,128)(2,1)}, u32[]{:S(2)}) %copy-start.1) | copy-done | bytes 524312
  3.2 0.0 copy-start.2
  3.2 0.9 %copy-done.2 = bf16[32,2048]{1,0:T(8,128)(2,1)S(1)} copy-done((bf16[32,2048]{1,0:T(8,128)(2,1)S(1)}, bf16[32,2048]{1,0:T(8,128)(2,1)}, u32[]{:S(2)}) %copy-start.2) | copy-done | bytes 131096
  4.1 32.0 %shard_map.46 = f32[8,120]{1,0:T(8,128)S(1)} custom-call(bf16[8,120,2048]{2,1,0:T(8,128)(2,1)S(1)} %bitcast.2, bf16[32,2048]{1,0:T(8,128)(2,1)S(1)} %copy-done.2, bf16[4,256,2048]{2,1,0:T(8,128)(2,1)} %bitcast.3, bf16[1024,256]{1,0:T(8,128)(2,1)S(1)} %copy-done.1), custom_call_target="tpu_custom_call" | custom-call | tf_op jit(solution)/shard_map/pallas_call | solution.py:162
  36.1 0.6 %copy.6 = f32[8,120]{1,0:T(8,128)} copy(f32[8,120]{1,0:T(8,128)S(1)} %shard_map.46) | data formatting | bytes 7680
Async XLA Ops:
  0.0 2.1 %copy-start = (bf16[960,2048]{1,0:T(8,128)(2,1)S(1)}, bf16[960,2048]{1,0:T(8,128)(2,1)}, u32[]{:S(2)}) copy-start(bf16[960,2048]{1,0:T(8,128)(2,1)} %param.4) | copy-start | bytes 11796484
  2.1 1.0 %copy-start.1 = (bf16[1024,256]{1,0:T(8,128)(2,1)S(1)}, bf16[1024,256]{1,0:T(8,128)(2,1)}, u32[]{:S(2)}) copy-start(bf16[1024,256]{1,0:T(8,128)(2,1)} %w_hbm.1) | copy-start | bytes 1572868
  3.2 0.9 %copy-start.2 = (bf16[32,2048]{1,0:T(8,128)(2,1)S(1)}, bf16[32,2048]{1,0:T(8,128)(2,1)}, u32[]{:S(2)}) copy-start(bf16[32,2048]{1,0:T(8,128)(2,1)} %q_hbm.1) | copy-start | bytes 393220

commit v3 on v2

--- a/solution.py
+++ b/solution.py
@@ -19,7 +19,7 @@
 def kernel(
     n_layer, n_land, factor,
     g_hbm, q_hbm, l_hbm, w_hbm, out_ref,
-    g_buf, q_buf, l_buf, w_buf, load_sem,
+    g_buf, p_buf, q_buf, l_buf, w_buf, load_sem,
     qs, qr, hs, hr, us, ur, bs, br, ss, sr, fs, fr,
     layer_send, layer_recv, land_send, land_recv,
 ):
@@ -76,6 +76,12 @@
         return copies
 
     sent = []
+    each = p_buf.shape[1]
+
+    def project(b):
+        part = dot(g_buf[...], l_buf[b], NT)
+        for i in range(n_layer):
+            p_buf[i, :, b * width:(b + 1) * width] = part[i * each:(i + 1) * each].astype(HALF)
 
     loads[0].wait()
     rows = qs.shape[1]
@@ -89,6 +95,8 @@
     pl.semaphore_wait(barrier, n_layer + n_land - 2)
 
     copies = over_layer(0, lambda p: qs.at[p], lambda k: qr.at[k - 1])
+    loads[2 + n_blocks].wait()
+    project(0)
     total = qs[layer].astype(FULL)
     for k, copy in enumerate(copies):
         copy.wait_recv()
@@ -97,6 +105,7 @@
 
     hs[...] = total
     copies = over_land(0, lambda p: hs, lambda k: hr.at[k - 1])
+    project(1)
     for k, copy in enumerate(copies):
         copy.wait_recv()
         total += hr[k]
@@ -107,6 +116,7 @@
     back = dot(white, w_buf[...], NT)
     us[...] = back
     copies = over_land(1, lambda p: us, lambda k: ur.at[k - 1])
+    project(2)
     for k, copy in enumerate(copies):
         copy.wait_recv()
         back += ur[k]
@@ -115,19 +125,14 @@
     bs[...] = back.astype(HALF)
     copies = over_layer(1, lambda p: bs, lambda k: br.at[layer])
     br[layer] = bs[...]
-    loads[2 + n_blocks].wait()
+    project(3)
     for copy in copies:
         copy.wait_recv()
     sent += copies
 
     folded = jnp.concatenate([br[i].astype(FULL) for i in range(n_layer)], axis=0).astype(HALF)
-    spread = jnp.zeros((folded.shape[0], l_buf.shape[2]), FULL)
-    for b in range(n_blocks):
-        spread += dot(folded[:, b * width:(b + 1) * width], l_buf[b], NN)
-    spread = spread.astype(HALF)
-
     for i in range(n_layer):
-        ss[i] = (dot(spread, g_buf[i], NT) * factor).astype(HALF)
+        ss[i] = (dot(folded, p_buf[i], NT) * factor).astype(HALF)
     copies = over_layer(2, lambda p: ss.at[p], lambda k: sr.at[k - 1])
     score = ss[layer].astype(FULL)
     for k, copy in enumerate(copies):
@@ -158,14 +163,15 @@
     n_mark = landmarks.shape[0]
     n_blocks = 4
     each, rows, share = n_rows // n_layer, n_query // n_layer, n_query // n_land
-    any_space = pl.BlockSpec(memory_space=pl.ANY)
+    any_space = pl.BlockSpec(memory_space=pltpu.HBM)
     return pl.pallas_call(
         functools.partial(kernel, n_layer, n_land, n_mark ** (-0.5)),
         out_shape=jax.ShapeDtypeStruct((share, each), FULL),
         in_specs=[any_space] * 4,
         out_specs=pl.BlockSpec(memory_space=pltpu.VMEM),
         scratch_shapes=[
-            pltpu.VMEM((n_layer, each, width), HALF),
+            pltpu.VMEM((n_rows, width), HALF),
+            pltpu.VMEM((n_layer, each, n_mark), HALF),
             pltpu.VMEM((n_query, width), HALF),
             pltpu.VMEM((n_blocks, n_mark // n_blocks, width), HALF),
             pltpu.VMEM(whitening.shape, HALF),
@@ -188,10 +194,10 @@
             pltpu.SemaphoreType.DMA((3, n_land - 1)),
         ],
         compiler_params=pltpu.CompilerParams(
-            collective_id=0, has_side_effects=True, vmem_limit_bytes=48 << 20
+            collective_id=0, has_side_effects=True, vmem_limit_bytes=63 << 20
         ),
     )(
-        gradients.reshape(n_layer, each, width),
+        gradients,
         queries,
         landmarks.reshape(n_blocks, n_mark // n_blocks, width),
         whitening,

time: 36.9 us -> 32.6 us (0.88)
  local copies, waits for them, and re-layouts: 4.65 us -> 1.28 us
  Pallas kernels: 32 us -> 31.2 us
    unnamed x7 -> x1, local copies, waits for them, and re-layouts: 4.65 us -> 1.28 us
    pallas_call x1, Pallas kernels: 32 us -> 31.2 us  [fused(): pl.pallas_call(functools.partial(kernel, n_layer, n_land, n_mark ** (-0.5...]
where the time goes in v3:
time: 32.6 us; the launch traced here: 32.4 us
  Pallas kernels  31.2 us (96%)
  local copies, waits for them, and re-layouts  1.28 us (4%)
    pallas_call x1, Pallas kernels, fused(): pl.pallas_call(functools.partial(kernel, n_layer, n_land, n_mark ** (-0.5...  31.2 us
    unnamed x1, local copies, waits for them, and re-layouts  1.28 us

profile of v3, /device:TPU:0, one launch (start us, length us, event | category | flops | bytes accessed | tf_op | source)
XLA Modules:
  0.0 32.4 jit_solution(16766831366574769229)
XLA Ops:
  0.0 31.2 %shard_map.46 = f32[8,120]{1,0:T(8,128)} custom-call(bf16[960,2048]{1,0:T(8,128)(2,1)} %g_hbm.1, bf16[32,2048]{1,0:T(8,128)(2,1)} %q_hbm.1, bf16[4,256,2048]{2,1,0:T(8,128)(2,1)} %bitcast.1, bf16[1024,256]{1,0:T(8,128)(2,1)} %w_hbm.1), custom_call_target="tpu_custom_call" | custom-call | tf_op jit(solution)/shard_map/pallas_call | solution.py:167
  31.2 1.3 %copy.6 = f32[8,120]{1,0:T(8,128)} copy(f32[8,120]{1,0:T(8,128)} %shard_map.46) | data formatting | bytes 7680

commit v4 on v3

--- a/solution.py
+++ b/solution.py
@@ -20,8 +20,8 @@
     n_layer, n_land, factor,
     g_hbm, q_hbm, l_hbm, w_hbm, out_ref,
     g_buf, p_buf, q_buf, l_buf, w_buf, load_sem,
-    qs, qr, hs, hr, us, ur, bs, br, ss, sr, fs, fr,
-    layer_send, layer_recv, land_send, land_recv,
+    qs, qr, hs, hr, us, ur, bs, br, ss, sr,
+    layer_send, layer_recv, land_send, land_recv, score_send, score_recv,
 ):
     layer = lax.axis_index("layer")
     land = lax.axis_index("land")
@@ -131,24 +131,27 @@
     sent += copies
 
     folded = jnp.concatenate([br[i].astype(FULL) for i in range(n_layer)], axis=0).astype(HALF)
-    for i in range(n_layer):
-        ss[i] = (dot(folded, p_buf[i], NT) * factor).astype(HALF)
-    copies = over_layer(2, lambda p: ss.at[p], lambda k: sr.at[k - 1])
-    score = ss[layer].astype(FULL)
-    for k, copy in enumerate(copies):
-        copy.wait_recv()
-        score += sr[k].astype(FULL)
-    sent += copies
-
-    share = fs.shape[1]
-    for j in range(n_land):
-        fs[j] = score[j * share:(j + 1) * share]
-    copies = over_land(2, lambda p: fs.at[p], lambda k: fr.at[k - 1])
-    result = fs[land]
-    for k, copy in enumerate(copies):
-        copy.wait_recv()
-        result += fr[k]
-    sent += copies
+    share = out_ref.shape[0]
+    copies = []
+    for k in list(range(1, n_layer)) + [0]:
+        peer = layer_peer(k)
+        block = dot(folded, p_buf[peer], NT) * factor
+        for j in range(n_land):
+            ss[k, j] = block[j * share:(j + 1) * share].astype(HALF)
+        for kj in range(n_land):
+            if k or kj:
+                other = land_peer(kj)
+                copy = pltpu.make_async_remote_copy(
+                    src_ref=ss.at[k, other], dst_ref=sr.at[k, kj],
+                    send_sem=score_send.at[k, kj], recv_sem=score_recv.at[k, kj],
+                    device_id=(peer, other), device_id_type=pl.DeviceIdType.MESH)
+                copy.start()
+                copies.append((k, kj, copy))
+    result = ss[0, land].astype(FULL)
+    for k, kj, copy in copies[::-1]:
+        copy.wait_recv()
+        result += sr[k, kj].astype(FULL)
+        sent.append(copy)
     out_ref[...] = result
 
     for copy in sent:
@@ -184,14 +187,14 @@
             pltpu.VMEM((n_land - 1, rows, n_mark), FULL),
             pltpu.VMEM((rows, n_mark), HALF),
             pltpu.VMEM((n_layer, rows, n_mark), HALF),
-            pltpu.VMEM((n_layer, n_query, each), HALF),
-            pltpu.VMEM((n_layer - 1, n_query, each), HALF),
-            pltpu.VMEM((n_land, share, each), FULL),
-            pltpu.VMEM((n_land - 1, share, each), FULL),
-            pltpu.SemaphoreType.DMA((3, n_layer - 1)),
-            pltpu.SemaphoreType.DMA((3, n_layer - 1)),
-            pltpu.SemaphoreType.DMA((3, n_land - 1)),
-            pltpu.SemaphoreType.DMA((3, n_land - 1)),
+            pltpu.VMEM((n_layer, n_land, share, each), HALF),
+            pltpu.VMEM((n_layer, n_land, share, each), HALF),
+            pltpu.SemaphoreType.DMA((2, n_layer - 1)),
+            pltpu.SemaphoreType.DMA((2, n_layer - 1)),
+            pltpu.SemaphoreType.DMA((2, n_land - 1)),
+            pltpu.SemaphoreType.DMA((2, n_land - 1)),
+            pltpu.SemaphoreType.DMA((n_layer, n_land)),
+            pltpu.SemaphoreType.DMA((n_layer, n_land)),
         ],
         compiler_params=pltpu.CompilerParams(
             collective_id=0, has_side_effects=True, vmem_limit_bytes=63 << 20

time: 32.6 us -> 30.4 us (0.933)
  Pallas kernels: 31.2 us -> 28.9 us
    pallas_call x1, Pallas kernels: 31.2 us -> 28.9 us  [fused(): pl.pallas_call(functools.partial(kernel, n_layer, n_land, n_mark ** (-0.5...]
where the time goes in v4:
time: 30.4 us; the launch traced here: 30.2 us
  Pallas kernels  28.9 us (95%)
  local copies, waits for them, and re-layouts  1.28 us (4%)
    pallas_call x1, Pallas kernels, fused(): pl.pallas_call(functools.partial(kernel, n_layer, n_land, n_mark ** (-0.5...  28.9 us
    unnamed x1, local copies, waits for them, and re-layouts  1.28 us

profile of v4, /device:TPU:0, one launch (start us, length us, event | category | flops | bytes accessed | tf_op | source)
XLA Modules:
  0.0 30.2 jit_solution(9210645887178483601)
XLA Ops:
  0.0 28.9 %shard_map.46 = f32[8,120]{1,0:T(8,128)} custom-call(bf16[960,2048]{1,0:T(8,128)(2,1)} %g_hbm.1, bf16[32,2048]{1,0:T(8,128)(2,1)} %q_hbm.1, bf16[4,256,2048]{2,1,0:T(8,128)(2,1)} %bitcast.1, bf16[1024,256]{1,0:T(8,128)(2,1)} %w_hbm.1), custom_call_target="tpu_custom_call" | custom-call | tf_op jit(solution)/shard_map/pallas_call | solution.py:170
  28.9 1.3 %copy.6 = f32[8,120]{1,0:T(8,128)} copy(f32[8,120]{1,0:T(8,128)} %shard_map.46) | data formatting | bytes 7680

commit v5 on v4

--- a/solution.py
+++ b/solution.py
@@ -49,9 +49,11 @@
         pl.semaphore_signal(barrier, inc=1, device_id=(layer, land_peer(k)),
                             device_id_type=pl.DeviceIdType.MESH)
 
+    far = sorted(range(1, n_layer), key=lambda k: -abs(2 * k - n_layer))
+
     def over_layer(phase, source, target):
-        copies = []
-        for k in range(1, n_layer):
+        copies = {}
+        for k in far:
             peer = layer_peer(k)
             copy = pltpu.make_async_remote_copy(
                 src_ref=source(peer), dst_ref=target(k),
@@ -59,8 +61,8 @@
                 recv_sem=layer_recv.at[phase, k - 1],
                 device_id=(peer, land), device_id_type=pl.DeviceIdType.MESH)
             copy.start()
-            copies.append(copy)
-        return copies
+            copies[k] = copy
+        return [copies[k] for k in range(1, n_layer)]
 
     def over_land(phase, source, target):
         copies = []
@@ -103,23 +105,23 @@
         total += qr[k].astype(FULL)
     sent += copies
 
-    hs[...] = total
+    hs[...] = total.astype(HALF)
     copies = over_land(0, lambda p: hs, lambda k: hr.at[k - 1])
     project(1)
     for k, copy in enumerate(copies):
         copy.wait_recv()
-        total += hr[k]
+        total += hr[k].astype(FULL)
     sent += copies
 
     loads[1 + n_blocks].wait()
     white = dot(total.astype(HALF), w_buf[...], NN).astype(HALF)
     back = dot(white, w_buf[...], NT)
-    us[...] = back
+    us[...] = back.astype(HALF)
     copies = over_land(1, lambda p: us, lambda k: ur.at[k - 1])
     project(2)
     for k, copy in enumerate(copies):
         copy.wait_recv()
-        back += ur[k]
+        back += ur[k].astype(FULL)
     sent += copies
 
     bs[...] = back.astype(HALF)
@@ -133,7 +135,7 @@
     folded = jnp.concatenate([br[i].astype(FULL) for i in range(n_layer)], axis=0).astype(HALF)
     share = out_ref.shape[0]
     copies = []
-    for k in list(range(1, n_layer)) + [0]:
+    for k in far + [0]:
         peer = layer_peer(k)
         block = dot(folded, p_buf[peer], NT) * factor
         for j in range(n_land):
@@ -181,10 +183,10 @@
             pltpu.SemaphoreType.DMA((n_blocks + 3,)),
             pltpu.VMEM((n_layer, rows, n_mark), HALF),
             pltpu.VMEM((n_layer - 1, rows, n_mark), HALF),
-            pltpu.VMEM((rows, n_mark), FULL),
-            pltpu.VMEM((n_land - 1, rows, n_mark), FULL),
-            pltpu.VMEM((rows, n_mark), FULL),
-            pltpu.VMEM((n_land - 1, rows, n_mark), FULL),
+            pltpu.VMEM((rows, n_mark), HALF),
+            pltpu.VMEM((n_land - 1, rows, n_mark), HALF),
+            pltpu.VMEM((rows, n_mark), HALF),
+            pltpu.VMEM((n_land - 1, rows, n_mark), HALF),
             pltpu.VMEM((rows, n_mark), HALF),
             pltpu.VMEM((n_layer, rows, n_mark), HALF),
             pltpu.VMEM((n_layer, n_land, share, each), HALF),

time: 30.4 us -> 30.3 us (level)
  no operation moved by 1% of the time
where the time goes in v5:
time: 30.3 us; the launch traced here: 30.1 us
  Pallas kernels  28.9 us (95%)
  local copies, waits for them, and re-layouts  1.28 us (4%)
    pallas_call x1, Pallas kernels, fused(): pl.pallas_call(functools.partial(kernel, n_layer, n_land, n_mark ** (-0.5...  28.9 us
    unnamed x1, local copies, waits for them, and re-layouts  1.28 us

profile of v5, /device:TPU:0, one launch (start us, length us, event | category | flops | bytes accessed | tf_op | source)
XLA Modules:
  0.0 30.1 jit_solution(7408260559318135289)
XLA Ops:
  0.0 28.9 %shard_map.46 = f32[8,120]{1,0:T(8,128)} custom-call(bf16[960,2048]{1,0:T(8,128)(2,1)} %g_hbm.1, bf16[32,2048]{1,0:T(8,128)(2,1)} %q_hbm.1, bf16[4,256,2048]{2,1,0:T(8,128)(2,1)} %bitcast.1, bf16[1024,256]{1,0:T(8,128)(2,1)} %w_hbm.1), custom_call_target="tpu_custom_call" | custom-call | tf_op jit(solution)/shard_map/pallas_call | solution.py:172
  28.9 1.3 %copy.6 = f32[8,120]{1,0:T(8,128)} copy(f32[8,120]{1,0:T(8,128)} %shard_map.46) | data formatting | bytes 7680
